TPU v7x, 256 devices: a whole 4x4x8 slice. The times are simulated.
256 devices in a mesh: blk: 8 (over y, core), wide: 32 (over x, z).
Axes of the slice: x: 4, y: 4, z: 8, core: 2. Of those that a mesh axis runs over, the one named last changes fastest.
Arguments:
- amplitudes: bfloat16 [2048, 262144], P(('blk', 'wide')), may hold values from -6 to 6
- integrals: bfloat16 [32, 256, 128, 128], P('wide', 'blk'), may hold values from -0.03125 to 0.03125
- out_tile: int32 [32, 256], P('wide'), may hold values from 0 to 31, as said below
- cd_slot: int32 [32, 256], P('wide'), may hold values from 0 to 63, as said below
Outputs:
- ladder: bfloat16 [2048, 4096], P('blk', 'wide')
Inputs may be any that keep to these rules, and one draw needn't show every extreme that they name: `out_tile`: output tile a lies in sector a mod 8. In each group every one of its 64 contracted tiles appears in exactly 4 entries, once with each output tile of one sector, the sector drawn for that tile; entries are in no particular order. `cd_slot`: see out_tile.
All inputs are finite; a program needn't handle non-finite values.
Results may differ from a plain program's by a relative error of at most 0.001.
Values may be sent and summed in bfloat16 or wider, within the bound.
No kernel may reach another device: no remote copies, remote signals or barrier semaphores. Data moves between devices by JAX's collectives and lax.ppermute only.
A program may use at most 192 MiB of HBM per device.

v0:
```python
import jax
import jax.numpy as jnp
from jax import lax
from jax.sharding import PartitionSpec as P

SECTORS = 8
A_PER = 4


def on_device(amplitudes, integrals, out_tile, cd_slot):
    n_out = SECTORS * A_PER
    tile_size = integrals.shape[2]
    exchanged = lax.all_to_all(amplitudes, "wide", split_axis=1, concat_axis=0, tiled=True)
    rows = exchanged.shape[0]
    columns = exchanged.reshape(rows, -1, tile_size)
    n_slots = columns.shape[1]
    outs_group = out_tile[0]
    slots_group = cd_slot[0]

    def accumulate(carry, piece, start):
        count = piece.shape[1]
        out_block = lax.dynamic_slice_in_dim(outs_group, start, count, 0)
        slot_block = lax.dynamic_slice_in_dim(slots_group, start, count, 0)
        slot_onehot = (slot_block[:, None] == jnp.arange(n_slots, dtype=jnp.int32)[None, :]).astype(
            jnp.bfloat16
        )
        picked = jnp.einsum(
            "kc,rct->rkt", slot_onehot, columns, preferred_element_type=jnp.float32
        ).astype(jnp.bfloat16)
        products = jnp.einsum("rkt,ktu->rku", picked, piece[0], preferred_element_type=jnp.float32)
        out_onehot = (out_block[:, None] == jnp.arange(n_out, dtype=jnp.int32)[None, :]).astype(
            jnp.float32
        )
        placed = jnp.einsum("ka,rku->rau", out_onehot, products, precision=lax.Precision.HIGHEST)
        return carry + placed

    empty = jnp.zeros((rows, n_out, tile_size), jnp.float32)
    everything = lax.all_gather(integrals, "blk", axis=1, tiled=True)
    count = integrals.shape[1]

    def step(index, carry):
        first = index * count
        piece = lax.dynamic_slice_in_dim(everything, first, count, 1)
        return accumulate(carry, piece, first)

    partial_sum = lax.fori_loop(0, lax.axis_size("blk"), step, empty)
    flat = partial_sum.reshape(rows, n_out * tile_size)
    return lax.psum_scatter(flat, "wide", scatter_dimension=1, tiled=True).astype(jnp.bfloat16)


def solution(mesh):
    in_specs = (
        P(("blk", "wide"), None),
        P("wide", "blk", None, None),
        P("wide", None),
        P("wide", None),
    )
    out_specs = P("blk", "wide")
    return jax.shard_map(
        on_device, mesh=mesh, in_specs=in_specs, out_specs=out_specs, check_vma=False
    )
```

profile of v0, /device:TPU:8, one launch (start us, length us, event | category | flops | bytes accessed | tf_op | source)
XLA Modules:
  0.0 524.1 jit_solution(3979197923908216875)
XLA Ops:
  6.5 0.0 all-gather.2.cloned.1.call-start
  6.5 0.7 all-gather.2.cloned.1.call-update
  7.3 11.5 %all-to-all-start = ((bf16[8,32,8192]{2,0,1:T(8,128)(2,1)}), bf16[8,32,8192]{2,0,1:T(8,128)(2,1)}, u32[]{:S(2)}, u32[]{:S(2)}) async-start(bf16[8,32,8192]{2,0,1:T(8,128)(2,1)} %bitcast.50), calls=%async_computation | async-start | bytes 8388608 | tf_op jit(solution)/shard_map/all_to_all | solution.py:13
  18.7 0.0 reduce-scatter.2.cloned.1.call-start
  18.8 96.9 %all-to-all-done = bf16[8,32,8192]{2,0,1:T(8,128)(2,1)} async-done(((bf16[8,32,8192]{2,0,1:T(8,128)(2,1)}), bf16[8,32,8192]{2,0,1:T(8,128)(2,1)}, u32[]{:S(2)}, u32[]{:S(2)}) %all-to-all-start) | async-done | bytes 4194336 | tf_op jit(solution)/shard_map/all_to_all | solution.py:13
  115.7 0.0 copy-start
  115.7 0.0 copy-start.1
  115.7 5.4 %copy.9 = bf16[32,8,64,128]{3,2,1,0:T(8,128)(2,1)} copy(bf16[32,8,64,128]{3,1,2,0:T(8,128)(2,1)} %bitcast.13) | data formatting | bytes 8388608
  121.1 0.0 all-gather.2.cloned.1.call-done
  121.1 0.0 copy-done
  121.1 0.0 copy-done.1
  121.1 165.7 %while.14 = (s32[]{:T(128)}, f32[256,32,128]{2,1,0:T(8,128)}, bf16[1,256,128,128]{3,2,1,0:T(8,128)(2,1)}, s32[256]{0:T(256)S(1)}, bf16[256,64,128]{2,1,0:T(8,128...) while((s32[]{:T(128)}, f32[256,32,128]{2,1,0:T(8,128)}, ...), condition=%wide.region_1.0_spmd.clone, body=%wide.region_0.0_spmd.clone.sunk | while | flops 807406592 | bytes 34603952 | solution.py:46
  121.1 0.1 dynamic_slice.33
  121.2 0.1 dynamic_slice.32
  121.3 2.9 fusion.32
  124.2 4.6 fusion.33
  128.8 5.5 %copy.20 = f32[32,128,256]{1,0,2:T(8,128)} copy(f32[32,128,256]{2,1,0:T(8,128)} %fusion.33) | data formatting | bytes 8388608 | tf_op jit(solution)/shard_map/while/body/eval_jaxpr/rkt,ktu->rku/dot_general | solution.py:30
  134.3 6.4 %bitcast_add_fusion.2 = f32[256,32,128]{2,1,0:T(8,128)} fusion(f32[256,32,128]{2,1,0:T(8,128)} %get-tuple-element.202, f32[32,128,256]{1,0,2:T(8,128)} %copy.20, pred[]{:T(512)S(6)} %compare.3, s32[32]{0:T(128)S(1)} %dynamic_slice.33), kind=kOutput, calls=%fused_computation.clone.1 | convolution fusion | flops 404751360 | bytes 12583041 | tf_op jit(solution)/shard_map/while/body/eval_jaxpr/ka,rku->rau/dot_general | solution.py:34
  140.7 0.1 dynamic_slice.33
  140.8 0.1 dynamic_slice.32
  140.9 2.9 fusion.32
  143.8 4.6 fusion.33
  148.4 5.5 %copy.20 = f32[32,128,256]{1,0,2:T(8,128)} copy(f32[32,128,256]{2,1,0:T(8,128)} %fusion.33) | data formatting | bytes 8388608 | tf_op jit(solution)/shard_map/while/body/eval_jaxpr/rkt,ktu->rku/dot_general | solution.py:30
  153.9 7.7 %bitcast_add_fusion.2 = f32[256,32,128]{2,1,0:T(8,128)} fusion(f32[256,32,128]{2,1,0:T(8,128)} %get-tuple-element.202, f32[32,128,256]{1,0,2:T(8,128)} %copy.20, pred[]{:T(512)S(6)} %compare.3, s32[32]{0:T(128)S(1)} %dynamic_slice.33), kind=kOutput, calls=%fused_computation.clone.1 | convolution fusion | flops 404751360 | bytes 12583041 | tf_op jit(solution)/shard_map/while/body/eval_jaxpr/ka,rku->rau/dot_general | solution.py:34
  161.6 0.1 dynamic_slice.33
  161.7 0.1 dynamic_slice.32
  161.7 2.9 fusion.32
  164.7 4.6 fusion.33
  169.3 5.5 %copy.20 = f32[32,128,256]{1,0,2:T(8,128)} copy(f32[32,128,256]{2,1,0:T(8,128)} %fusion.33) | data formatting | bytes 8388608 | tf_op jit(solution)/shard_map/while/body/eval_jaxpr/rkt,ktu->rku/dot_general | solution.py:30
  174.7 7.7 %bitcast_add_fusion.2 = f32[256,32,128]{2,1,0:T(8,128)} fusion(f32[256,32,128]{2,1,0:T(8,128)} %get-tuple-element.202, f32[32,128,256]{1,0,2:T(8,128)} %copy.20, pred[]{:T(512)S(6)} %compare.3, s32[32]{0:T(128)S(1)} %dynamic_slice.33), kind=kOutput, calls=%fused_computation.clone.1 | convolution fusion | flops 404751360 | bytes 12583041 | tf_op jit(solution)/shard_map/while/body/eval_jaxpr/ka,rku->rau/dot_general | solution.py:34
  182.5 0.1 dynamic_slice.33
  182.5 0.1 dynamic_slice.32
  182.6 2.9 fusion.32
  185.5 4.6 fusion.33
  190.1 5.5 %copy.20 = f32[32,128,256]{1,0,2:T(8,128)} copy(f32[32,128,256]{2,1,0:T(8,128)} %fusion.33) | data formatting | bytes 8388608 | tf_op jit(solution)/shard_map/while/body/eval_jaxpr/rkt,ktu->rku/dot_general | solution.py:30
  195.6 7.7 %bitcast_add_fusion.2 = f32[256,32,128]{2,1,0:T(8,128)} fusion(f32[256,32,128]{2,1,0:T(8,128)} %get-tuple-element.202, f32[32,128,256]{1,0,2:T(8,128)} %copy.20, pred[]{:T(512)S(6)} %compare.3, s32[32]{0:T(128)S(1)} %dynamic_slice.33), kind=kOutput, calls=%fused_computation.clone.1 | convolution fusion | flops 404751360 | bytes 12583041 | tf_op jit(solution)/shard_map/while/body/eval_jaxpr/ka,rku->rau/dot_general | solution.py:34
  203.3 0.1 dynamic_slice.33
  203.4 0.1 dynamic_slice.32
  203.5 2.9 fusion.32
  206.4 4.6 fusion.33
  211.0 5.5 %copy.20 = f32[32,128,256]{1,0,2:T(8,128)} copy(f32[32,128,256]{2,1,0:T(8,128)} %fusion.33) | data formatting | bytes 8388608 | tf_op jit(solution)/shard_map/while/body/eval_jaxpr/rkt,ktu->rku/dot_general | solution.py:30
  216.5 7.7 %bitcast_add_fusion.2 = f32[256,32,128]{2,1,0:T(8,128)} fusion(f32[256,32,128]{2,1,0:T(8,128)} %get-tuple-element.202, f32[32,128,256]{1,0,2:T(8,128)} %copy.20, pred[]{:T(512)S(6)} %compare.3, s32[32]{0:T(128)S(1)} %dynamic_slice.33), kind=kOutput, calls=%fused_computation.clone.1 | convolution fusion | flops 404751360 | bytes 12583041 | tf_op jit(solution)/shard_map/while/body/eval_jaxpr/ka,rku->rau/dot_general | solution.py:34
  224.2 0.1 dynamic_slice.33
  224.3 0.1 dynamic_slice.32
  224.3 2.9 fusion.32
  227.3 4.6 fusion.33
  231.9 5.5 %copy.20 = f32[32,128,256]{1,0,2:T(8,128)} copy(f32[32,128,256]{2,1,0:T(8,128)} %fusion.33) | data formatting | bytes 8388608 | tf_op jit(solution)/shard_map/while/body/eval_jaxpr/rkt,ktu->rku/dot_general | solution.py:30
  237.3 7.7 %bitcast_add_fusion.2 = f32[256,32,128]{2,1,0:T(8,128)} fusion(f32[256,32,128]{2,1,0:T(8,128)} %get-tuple-element.202, f32[32,128,256]{1,0,2:T(8,128)} %copy.20, pred[]{:T(512)S(6)} %compare.3, s32[32]{0:T(128)S(1)} %dynamic_slice.33), kind=kOutput, calls=%fused_computation.clone.1 | convolution fusion | flops 404751360 | bytes 12583041 | tf_op jit(solution)/shard_map/while/body/eval_jaxpr/ka,rku->rau/dot_general | solution.py:34
  245.1 0.1 dynamic_slice.33
  245.1 0.1 dynamic_slice.32
  245.2 2.9 fusion.32
  248.2 4.6 fusion.33
  252.7 5.5 %copy.20 = f32[32,128,256]{1,0,2:T(8,128)} copy(f32[32,128,256]{2,1,0:T(8,128)} %fusion.33) | data formatting | bytes 8388608 | tf_op jit(solution)/shard_map/while/body/eval_jaxpr/rkt,ktu->rku/dot_general | solution.py:30
  258.2 7.7 %bitcast_add_fusion.2 = f32[256,32,128]{2,1,0:T(8,128)} fusion(f32[256,32,128]{2,1,0:T(8,128)} %get-tuple-element.202, f32[32,128,256]{1,0,2:T(8,128)} %copy.20, pred[]{:T(512)S(6)} %compare.3, s32[32]{0:T(128)S(1)} %dynamic_slice.33), kind=kOutput, calls=%fused_computation.clone.1 | convolution fusion | flops 404751360 | bytes 12583041 | tf_op jit(solution)/shard_map/while/body/eval_jaxpr/ka,rku->rau/dot_general | solution.py:34
  265.9 0.1 dynamic_slice.33
  266.0 0.1 dynamic_slice.32
  266.1 2.9 fusion.32
  269.0 4.6 fusion.33
  273.6 5.5 %copy.20 = f32[32,128,256]{1,0,2:T(8,128)} copy(f32[32,128,256]{2,1,0:T(8,128)} %fusion.33) | data formatting | bytes 8388608 | tf_op jit(solution)/shard_map/while/body/eval_jaxpr/rkt,ktu->rku/dot_general | solution.py:30
  279.1 7.7 %bitcast_add_fusion.2 = f32[256,32,128]{2,1,0:T(8,128)} fusion(f32[256,32,128]{2,1,0:T(8,128)} %get-tuple-element.202, f32[32,128,256]{1,0,2:T(8,128)} %copy.20, pred[]{:T(512)S(6)} %compare.3, s32[32]{0:T(128)S(1)} %dynamic_slice.33), kind=kOutput, calls=%fused_computation.clone.1 | convolution fusion | flops 404751360 | bytes 12583041 | tf_op jit(solution)/shard_map/while/body/eval_jaxpr/ka,rku->rau/dot_general | solution.py:34
  286.8 7.9 %copy.16 = f32[32,8,32,128]{3,1,2,0:T(8,128)} copy(f32[32,8,32,128]{3,2,1,0:T(8,128)} %bitcast.47) | data formatting | bytes 8388608
  294.7 0.0 reduce-scatter.2.cloned.1.call-update
  294.7 221.0 %reduce-scatter.2.cloned.1.call-done = f32[256,128]{1,0:T(8,128)} async-done(((f32[256,4096]{1,0:T(8,128)}), f32[256,128]{1,0:T(8,128)}) %reduce-scatter.2.cloned.1.call-update) | async-done | bytes 131088 | tf_op jit(solution)/shard_map/reduce_scatter | solution.py:48
  515.7 1.5 convert_element_type.19
  (1 shorter events, 0.0 us)
Async XLA Ops:
  6.5 114.6 %all-gather.2.cloned.1.call-start = ((), (), s32[]{:S(2)}) async-start(), calls=%async_computation.2 | async-start | bytes 9437184 | tf_op jit(solution)/shard_map/all_gather | solution.py:38
  7.3 108.5 %all-to-all-start = ((bf16[8,32,8192]{2,0,1:T(8,128)(2,1)}), bf16[8,32,8192]{2,0,1:T(8,128)(2,1)}, u32[]{:S(2)}, u32[]{:S(2)}) async-start(bf16[8,32,8192]{2,0,1:T(8,128)(2,1)} %bitcast.50), calls=%async_computation | async-start | bytes 8388608 | tf_op jit(solution)/shard_map/all_to_all | solution.py:13
  18.7 497.0 %reduce-scatter.2.cloned.1.call-start = ((), (), s32[]{:S(2)}) async-start(), calls=%async_computation.3 | async-start | bytes 4325376 | tf_op jit(solution)/shard_map/reduce_scatter | solution.py:48
  115.7 5.4 %copy-start = (s32[1,256]{1,0:T(1,128)S(1)}, s32[1,256]{1,0:T(1,128)}, u32[]{:S(2)}) copy-start(s32[1,256]{1,0:T(1,128)} %param.9) | copy-start | bytes 3076
  115.7 5.4 %copy-start.1 = (s32[1,256]{1,0:T(1,128)S(1)}, s32[1,256]{1,0:T(1,128)}, u32[]{:S(2)}) copy-start(s32[1,256]{1,0:T(1,128)} %param.8) | copy-start | bytes 3076
Sparse Core Ops, SparseCore 0:
  9.2 54.2 all-gather.1
  294.8 220.8 reduce-scatter.1
where the time goes:
time: 526 us; the launch traced here: 524 us
  waiting for transfers between devices  319 us (61%)
  matrix products  121 us (23%)
  local copies, waits for them, and re-layouts  58.2 us (11%)
  between operations  13.4 us (3%)
  starting transfers between devices  11.5 us (2%)
    reduce_scatter x1, waiting for transfers between devices, on_device(): lax.psum_scatter(flat, 'wide', scatter_dimension=1, tiled=True)  221 us
    all_to_all x1, waiting for transfers between devices, on_device(): lax.all_to_all(amplitudes, 'wide', split_axis=1, concat_axis=0, tiled=True)  96.9 us
    dot_general x8, matrix products, accumulate(): jnp.einsum('ka,rku->rau', out_onehot, products, precision=lax.Precision.H...  60.4 us
    dot_general x8, local copies, waits for them, and re-layouts, accumulate(): jnp.einsum('rkt,ktu->rku', picked, piece[0], preferred_element_type=jnp.f...  43.7 us
    dot_general x8, matrix products, accumulate(): jnp.einsum('rkt,ktu->rku', picked, piece[0], preferred_element_type=jnp.f...  36.7 us
    dot_general x8, matrix products, accumulate(): jnp.einsum('kc,rct->rkt', slot_onehot, columns, preferred_element_type=jn...  23.5 us
    unnamed x6, local copies, waits for them, and re-layouts  13.3 us
    all_to_all x1, starting transfers between devices, on_device(): lax.all_to_all(amplitudes, 'wide', split_axis=1, concat_axis=0, tiled=True)  11.5 us
  transfers between devices with their start and end apart: 3, of which 2 were waited for; matrix products, arithmetic and copies ran while one was open for 1% of the time, Pallas kernels for 0%

commit v1 on v0

--- a/solution.py
+++ b/solution.py
@@ -5,12 +5,21 @@
 
 SECTORS = 8
 A_PER = 4
+finish_strings = lambda page: jnp.concatenate(
+    lax.all_to_all(
+        jnp.stack(jnp.split(page, lax.axis_size("wide"), axis=1), axis=0),
+        axis_name="wide",
+        split_axis=0,
+        concat_axis=0,
+    ),
+    axis=0,
+)
 
 
 def on_device(amplitudes, integrals, out_tile, cd_slot):
     n_out = SECTORS * A_PER
     tile_size = integrals.shape[2]
-    exchanged = lax.all_to_all(amplitudes, "wide", split_axis=1, concat_axis=0, tiled=True)
+    exchanged = finish_strings(amplitudes)
     rows = exchanged.shape[0]
     columns = exchanged.reshape(rows, -1, tile_size)
     n_slots = columns.shape[1]

time: 526 us -> 577 us (1.097)
  local copies, waits for them, and re-layouts: 58.2 us -> 108 us
    unnamed x6 -> x37, local copies, waits for them, and re-layouts: 13.3 us -> 62 us
  transfers between devices with their start and end apart: 3 -> 3, of which waited for: 2 -> 2; matrix products, arithmetic and copies ran while one was open for 1% -> 10% of each run, Pallas kernels for 0% -> 0%
where the time goes in v1:
time: 577 us; the launch traced here: 574 us
  waiting for transfers between devices  319 us (55%)
  matrix products  121 us (21%)
  local copies, waits for them, and re-layouts  108 us (19%)
  between operations  13.4 us (2%)
  starting transfers between devices  11.5 us (2%)
    reduce_scatter x1, waiting for transfers between devices, on_device(): lax.psum_scatter(flat, 'wide', scatter_dimension=1, tiled=True)  221 us
    all_to_all x1, waiting for transfers between devices, lax.all_to_all(jnp.stack(jnp.split(page, lax.axis_size('wide'), axis=1),...  97 us
    unnamed x37, local copies, waits for them, and re-layouts  62 us
    dot_general x8, matrix products, accumulate(): jnp.einsum('ka,rku->rau', out_onehot, products, precision=lax.Precision.H...  60.4 us
    dot_general x8, local copies, waits for them, and re-layouts, accumulate(): jnp.einsum('rkt,ktu->rku', picked, piece[0], preferred_element_type=jnp.f...  43.7 us
    dot_general x8, matrix products, accumulate(): jnp.einsum('rkt,ktu->rku', picked, piece[0], preferred_element_type=jnp.f...  36.7 us
    dot_general x8, matrix products, accumulate(): jnp.einsum('kc,rct->rkt', slot_onehot, columns, preferred_element_type=jn...  23.5 us
  transfers between devices with their start and end apart: 3, of which 2 were waited for; matrix products, arithmetic and copies ran while one was open for 10% of the time, Pallas kernels for 0%

profile of v1, /device:TPU:8, one launch (start us, length us, event | category | flops | bytes accessed | tf_op | source)
XLA Modules:
  0.0 574.5 jit_solution(13439096934357297630)
XLA Ops:
  7.3 1.6 bitcast_dynamic-update-slice_fusion.31
  10.4 1.6 bitcast_dynamic-update-slice_fusion.29
  15.1 1.6 bitcast_dynamic-update-slice_fusion.26
  16.7 1.6 bitcast_dynamic-update-slice_fusion.25
  18.2 1.6 bitcast_dynamic-update-slice_fusion.24
  19.8 1.6 bitcast_dynamic-update-slice_fusion.23
  21.4 1.6 bitcast_dynamic-update-slice_fusion.22
  22.9 1.6 bitcast_dynamic-update-slice_fusion.21
  24.5 1.6 bitcast_dynamic-update-slice_fusion.20
  26.1 1.6 bitcast_dynamic-update-slice_fusion.19
  27.7 1.6 bitcast_dynamic-update-slice_fusion.18
  29.3 1.6 bitcast_dynamic-update-slice_fusion.17
  30.8 1.6 bitcast_dynamic-update-slice_fusion.16
  32.4 1.6 bitcast_dynamic-update-slice_fusion.15
  34.0 1.6 bitcast_dynamic-update-slice_fusion.14
  35.6 1.6 bitcast_dynamic-update-slice_fusion.13
  37.2 1.6 bitcast_dynamic-update-slice_fusion.12
  38.7 1.6 bitcast_dynamic-update-slice_fusion.11
  40.3 1.6 bitcast_dynamic-update-slice_fusion.10
  41.9 1.6 bitcast_dynamic-update-slice_fusion.9
  46.6 1.6 bitcast_dynamic-update-slice_fusion.6
  48.1 1.6 bitcast_dynamic-update-slice_fusion.5
  49.7 1.6 bitcast_dynamic-update-slice_fusion.4
  51.3 1.6 bitcast_dynamic-update-slice_fusion.3
  54.4 1.6 bitcast_dynamic-update-slice_fusion.1
  55.9 1.6 bitcast_dynamic-update-slice_fusion
  57.5 11.5 %all-to-all-start = ((bf16[32,8,8192]{2,1,0:T(8,128)(2,1)}), bf16[32,8,8192]{2,1,0:T(8,128)(2,1)}, u32[]{:S(2)}, u32[]{:S(2)}) async-start(bf16[32,8,8192]{2,1,0:T(8,128)(2,1)} %bitcast_dynamic-update-slice_fusion), calls=%async_computation | async-start | bytes 8388608 | tf_op jit(solution)/shard_map/all_to_all | solution.py:9
  69.1 97.0 %all-to-all-done = bf16[32,8,8192]{2,1,0:T(8,128)(2,1)} async-done(((bf16[32,8,8192]{2,1,0:T(8,128)(2,1)}), bf16[32,8,8192]{2,1,0:T(8,128)(2,1)}, u32[]{:S(2)}, u32[]{:S(2)}) %all-to-all-start) | async-done | bytes 4194336 | tf_op jit(solution)/shard_map/all_to_all | solution.py:9
  166.1 5.4 copy.9
  171.5 165.7 %while.14 = (s32[]{:T(128)}, f32[256,32,128]{2,1,0:T(8,128)}, bf16[1,256,128,128]{3,2,1,0:T(8,128)(2,1)}, s32[256]{0:T(256)S(1)}, bf16[256,64,128]{2,1,0:T(8,128...) while((s32[]{:T(128)}, f32[256,32,128]{2,1,0:T(8,128)}, ...), condition=%wide.region_1.0_spmd.clone, body=%wide.region_0.0_spmd.clone.sunk | while | flops 807406592 | bytes 34603952 | solution.py:55
  171.7 2.9 fusion.32
  174.6 4.6 fusion.33
  179.2 5.5 copy.20
  184.7 6.4 %bitcast_add_fusion.2 = f32[256,32,128]{2,1,0:T(8,128)} fusion(f32[256,32,128]{2,1,0:T(8,128)} %get-tuple-element.202, f32[32,128,256]{1,0,2:T(8,128)} %copy.20, pred[]{:T(512)S(6)} %compare.3, s32[32]{0:T(128)S(1)} %dynamic_slice.33), kind=kOutput, calls=%fused_computation.clone.1 | convolution fusion | flops 404751360 | bytes 12583041 | tf_op jit(solution)/shard_map/while/body/eval_jaxpr/ka,rku->rau/dot_general | solution.py:43
  191.3 2.9 fusion.32
  194.2 4.6 fusion.33
  198.8 5.5 copy.20
  204.3 7.7 %bitcast_add_fusion.2 = f32[256,32,128]{2,1,0:T(8,128)} fusion(f32[256,32,128]{2,1,0:T(8,128)} %get-tuple-element.202, f32[32,128,256]{1,0,2:T(8,128)} %copy.20, pred[]{:T(512)S(6)} %compare.3, s32[32]{0:T(128)S(1)} %dynamic_slice.33), kind=kOutput, calls=%fused_computation.clone.1 | convolution fusion | flops 404751360 | bytes 12583041 | tf_op jit(solution)/shard_map/while/body/eval_jaxpr/ka,rku->rau/dot_general | solution.py:43
  212.1 2.9 fusion.32
  215.1 4.6 fusion.33
  219.7 5.5 copy.20
  225.1 7.7 %bitcast_add_fusion.2 = f32[256,32,128]{2,1,0:T(8,128)} fusion(f32[256,32,128]{2,1,0:T(8,128)} %get-tuple-element.202, f32[32,128,256]{1,0,2:T(8,128)} %copy.20, pred[]{:T(512)S(6)} %compare.3, s32[32]{0:T(128)S(1)} %dynamic_slice.33), kind=kOutput, calls=%fused_computation.clone.1 | convolution fusion | flops 404751360 | bytes 12583041 | tf_op jit(solution)/shard_map/while/body/eval_jaxpr/ka,rku->rau/dot_general | solution.py:43
  233.0 2.9 fusion.32
  236.0 4.6 fusion.33
  240.5 5.5 copy.20
  246.0 7.7 %bitcast_add_fusion.2 = f32[256,32,128]{2,1,0:T(8,128)} fusion(f32[256,32,128]{2,1,0:T(8,128)} %get-tuple-element.202, f32[32,128,256]{1,0,2:T(8,128)} %copy.20, pred[]{:T(512)S(6)} %compare.3, s32[32]{0:T(128)S(1)} %dynamic_slice.33), kind=kOutput, calls=%fused_computation.clone.1 | convolution fusion | flops 404751360 | bytes 12583041 | tf_op jit(solution)/shard_map/while/body/eval_jaxpr/ka,rku->rau/dot_general | solution.py:43
  253.9 2.9 fusion.32
  256.8 4.6 fusion.33
  261.4 5.5 copy.20
  266.9 7.7 %bitcast_add_fusion.2 = f32[256,32,128]{2,1,0:T(8,128)} fusion(f32[256,32,128]{2,1,0:T(8,128)} %get-tuple-element.202, f32[32,128,256]{1,0,2:T(8,128)} %copy.20, pred[]{:T(512)S(6)} %compare.3, s32[32]{0:T(128)S(1)} %dynamic_slice.33), kind=kOutput, calls=%fused_computation.clone.1 | convolution fusion | flops 404751360 | bytes 12583041 | tf_op jit(solution)/shard_map/while/body/eval_jaxpr/ka,rku->rau/dot_general | solution.py:43
  274.7 2.9 fusion.32
  277.7 4.6 fusion.33
  282.3 5.5 copy.20
  287.7 7.7 %bitcast_add_fusion.2 = f32[256,32,128]{2,1,0:T(8,128)} fusion(f32[256,32,128]{2,1,0:T(8,128)} %get-tuple-element.202, f32[32,128,256]{1,0,2:T(8,128)} %copy.20, pred[]{:T(512)S(6)} %compare.3, s32[32]{0:T(128)S(1)} %dynamic_slice.33), kind=kOutput, calls=%fused_computation.clone.1 | convolution fusion | flops 404751360 | bytes 12583041 | tf_op jit(solution)/shard_map/while/body/eval_jaxpr/ka,rku->rau/dot_general | solution.py:43
  295.6 2.9 fusion.32
  298.6 4.6 fusion.33
  303.1 5.5 copy.20
  308.6 7.7 %bitcast_add_fusion.2 = f32[256,32,128]{2,1,0:T(8,128)} fusion(f32[256,32,128]{2,1,0:T(8,128)} %get-tuple-element.202, f32[32,128,256]{1,0,2:T(8,128)} %copy.20, pred[]{:T(512)S(6)} %compare.3, s32[32]{0:T(128)S(1)} %dynamic_slice.33), kind=kOutput, calls=%fused_computation.clone.1 | convolution fusion | flops 404751360 | bytes 12583041 | tf_op jit(solution)/shard_map/while/body/eval_jaxpr/ka,rku->rau/dot_general | solution.py:43
  316.5 2.9 fusion.32
  319.4 4.6 fusion.33
  324.0 5.5 copy.20
  329.5 7.7 %bitcast_add_fusion.2 = f32[256,32,128]{2,1,0:T(8,128)} fusion(f32[256,32,128]{2,1,0:T(8,128)} %get-tuple-element.202, f32[32,128,256]{1,0,2:T(8,128)} %copy.20, pred[]{:T(512)S(6)} %compare.3, s32[32]{0:T(128)S(1)} %dynamic_slice.33), kind=kOutput, calls=%fused_computation.clone.1 | convolution fusion | flops 404751360 | bytes 12583041 | tf_op jit(solution)/shard_map/while/body/eval_jaxpr/ka,rku->rau/dot_general | solution.py:43
  337.2 7.9 %copy.16 = f32[32,8,32,128]{3,1,2,0:T(8,128)} copy(f32[32,8,32,128]{3,2,1,0:T(8,128)} %bitcast.109) | data formatting | bytes 8388608
  345.1 221.0 %reduce-scatter.2.cloned.1.call-done = f32[256,128]{1,0:T(8,128)} async-done(((f32[256,4096]{1,0:T(8,128)}), f32[256,128]{1,0:T(8,128)}) %reduce-scatter.2.cloned.1.call-update) | async-done | bytes 131088 | tf_op jit(solution)/shard_map/reduce_scatter | solution.py:57
  (33 shorter events, 12.9 us)
Async XLA Ops:
  6.5 165.0 %all-gather.2.cloned.1.call-start = ((), (), s32[]{:S(2)}) async-start(), calls=%async_computation.2 | async-start | bytes 9437184 | tf_op jit(solution)/shard_map/all_gather | solution.py:47
  57.5 108.6 %all-to-all-start = ((bf16[32,8,8192]{2,1,0:T(8,128)(2,1)}), bf16[32,8,8192]{2,1,0:T(8,128)(2,1)}, u32[]{:S(2)}, u32[]{:S(2)}) async-start(bf16[32,8,8192]{2,1,0:T(8,128)(2,1)} %bitcast_dynamic-update-slice_fusion), calls=%async_computation | async-start | bytes 8388608 | tf_op jit(solution)/shard_map/all_to_all | solution.py:9
  69.0 497.1 %reduce-scatter.2.cloned.1.call-start = ((), (), s32[]{:S(2)}) async-start(), calls=%async_computation.3 | async-start | bytes 4325376 | tf_op jit(solution)/shard_map/reduce_scatter | solution.py:57
  166.1 5.4 copy-start
  166.1 5.4 copy-start.1
Sparse Core Ops, SparseCore 0:
  9.2 54.2 all-gather.1
  345.3 220.7 reduce-scatter.1
